TPU v7x, 32 devices: a whole 2x2x4 slice. The times are simulated.
32 devices in a mesh: replica: 8 (over z, core), fsdp: 4 (over y, x).
Axes of the slice: x: 2, y: 2, z: 4, core: 2. Of those that a mesh axis runs over, the one named last changes fastest.
Arguments:
- acts: bfloat16 [1, 4096, 8192], P(None, ('replica', 'fsdp')), may hold values from -6 to 6
- key_cot: bfloat16 [1, 4096, 512], P(None, ('replica', 'fsdp')), may hold values from -0.29882812 to 0.29882812
- params: float32 [8192, 512], P('fsdp'), may hold values from -4 to 4
- moment_one: float32 [8192, 512], P('fsdp'), may hold values from -1.8 to 1.8
- moment_two: float32 [8192, 512], P('fsdp'), may hold values from 0.05 to 2
- outer_mom: float32 [8192, 512], P(('fsdp', 'replica')), may hold values from -1.8 to 1.8
Outputs:
- new_params: float32 [8192, 512], P(('fsdp', 'replica'))
- new_mom: float32 [8192, 512], P(('fsdp', 'replica'))
All inputs are finite; a program needn't handle non-finite values.
Results may differ from a plain program's by a relative error of at most 0.0007.
Values may be sent and summed in bfloat16 or wider, within the bound.
A program may use at most 64 MiB of HBM per device.

v0:
```python
import jax
import jax.numpy as jnp
from jax import lax
from jax.sharding import PartitionSpec as P

beta_one = 0.9
beta_two = 0.95
epsilon = 1e-08
inner_rate = 0.3
decay_rate = 0.1
outer_rate = 0.7
momentum = 0.9


def adamw_step(weights, first, second, gradient):
    first = beta_one * first + (1.0 - beta_one) * gradient
    second = beta_two * second + (1.0 - beta_two) * gradient * gradient
    weights = weights - inner_rate * (first / (jnp.sqrt(second) + epsilon) + decay_rate * weights)
    return (weights, first, second)


def per_device(acts, key_cot, params, moment_one, moment_two, outer_mom):
    micro_count = acts.shape[0]
    local_rows = params.shape[0]
    kv_width = key_cot.shape[2]
    sliced = acts[0]
    partials = lax.dot_general(
        sliced, key_cot[0], (((0,), (0,)), ((), ())), preferred_element_type=jnp.float32
    )
    stacked = lax.psum_scatter(
        partials.astype(jnp.bfloat16), "fsdp", scatter_dimension=0, tiled=True
    ).astype(jnp.float32)
    gradients = stacked.reshape(local_rows, micro_count, kv_width).transpose(1, 0, 2)
    weights, first, second = (params, moment_one, moment_two)
    replica_rows = local_rows // lax.axis_size("replica")
    row_offset = lax.axis_index("replica") * replica_rows
    weights, first, second = adamw_step(weights, first, second, gradients[micro_count - 1])
    summed = lax.psum_scatter(params - weights, "replica", scatter_dimension=0, tiled=True)
    drift_mean = summed / lax.axis_size("replica")
    anchor = lax.dynamic_slice_in_dim(params, row_offset, replica_rows, 0)
    new_mom = momentum * outer_mom + drift_mean
    new_params = anchor - outer_rate * (drift_mean + momentum * new_mom)
    return (new_params, new_mom)


def solution(mesh):
    return jax.shard_map(
        per_device,
        mesh=mesh,
        in_specs=(
            P(None, ("replica", "fsdp"), None),
            P(None, ("replica", "fsdp"), None),
            P("fsdp", None),
            P("fsdp", None),
            P("fsdp", None),
            P(("fsdp", "replica"), None),
        ),
        out_specs=(P(("fsdp", "replica"), None), P(("fsdp", "replica"), None)),
        check_vma=False,
    )
```

profile of v0, /device:TPU:0, one launch (start us, length us, event | category | flops | bytes accessed | tf_op | source)
XLA Modules:
  0.0 171.9 jit_solution(13716789579757409341)
XLA Ops:
  7.2 0.0 copy-start
  7.2 0.0 reduce-scatter.3.cloned.1.call-start
  7.2 1.5 copy-done
  8.8 6.5 %convolution_convert_fusion = bf16[8192,512]{1,0:T(8,128)(2,1)} fusion(bf16[1,128,8192]{2,1,0:T(8,128)(2,1)S(1)} %copy-done, bf16[1,128,512]{2,1,0:T(8,128)(2,1)} %param.7), kind=kOutput, calls=%fused_computation | convolution fusion | flops 1077936128 | bytes 10616832 | tf_op jit(solution)/shard_map/dot_general | solution.py:27
  15.3 0.0 reduce-scatter.3.cloned.1.call-update
  15.3 0.0 reduce-scatter.5.cloned.1.call-start
  15.3 89.1 %reduce-scatter.3.cloned.1.call-done = bf16[2048,512]{1,0:T(8,128)(2,1)} async-done(((bf16[8192,512]{1,0:T(8,128)(2,1)}), bf16[2048,512]{1,0:T(8,128)(2,1)}) %reduce-scatter.3.cloned.1.call-update) | async-done | bytes 2097168 | tf_op jit(solution)/shard_map/reduce_scatter | solution.py:30
  104.5 8.1 %subtract_subtract_fusion = f32[2048,512]{1,0:T(8,128)} fusion(f32[2048,512]{1,0:T(8,128)} %param.8, bf16[2048,512]{1,0:T(8,128)(2,1)} %reduce-scatter.3.cloned.1.call-done, f32[2048,512]{1,0:T(8,128)} %param.10, f32[2048,512]{1,0:T(8,128)} %param.9), kind=kLoop, calls=%fused_computation.1 | loop fusion | flops 15728640 | bytes 18874368 | tf_op jit(solution)/shard_map/sub | solution.py:38
  112.6 0.0 copy-start.1
  112.6 0.0 reduce-scatter.5.cloned.1.call-update
  112.6 50.1 %reduce-scatter.5.cloned.1.call-done = f32[256,512]{1,0:T(8,128)} async-done(((f32[2048,512]{1,0:T(8,128)}), f32[256,512]{1,0:T(8,128)}) %reduce-scatter.5.cloned.1.call-update) | async-done | bytes 524304 | tf_op jit(solution)/shard_map/reduce_scatter | solution.py:38
  162.7 0.0 copy-done.1
  162.7 2.3 %multiply_subtract_fusion = (f32[256,512]{1,0:T(8,128)}, f32[256,512]{1,0:T(8,128)}) fusion(f32[2048,512]{1,0:T(8,128)} %param.8, s32[]{:T(128)S(6)} %select_n.3, f32[256,512]{1,0:T(8,128)} %reduce-scatter.5.cloned.1.call-done, f32[256,512]{1,0:T(8,128)S(1)} %copy-done.1), kind=kLoop, calls=%fused_computation.12 | loop fusion | flops 917504 | bytes 2621444 | tf_op jit(solution)/shard_map/sub | solution.py:42
Async XLA Ops:
  7.2 1.6 copy-start
  7.2 97.3 %reduce-scatter.3.cloned.1.call-start = ((), (), s32[]{:S(2)}) async-start(), calls=%async_computation.2 | async-start | bytes 10485760 | tf_op jit(solution)/shard_map/reduce_scatter | solution.py:30
  15.3 147.4 %reduce-scatter.5.cloned.1.call-start = ((), (), s32[]{:S(2)}) async-start(), calls=%async_computation.3 | async-start | bytes 4718592 | tf_op jit(solution)/shard_map/reduce_scatter | solution.py:38
  112.6 50.1 %copy-start.1 = (f32[256,512]{1,0:T(8,128)S(1)}, f32[256,512]{1,0:T(8,128)}, u32[]{:S(2)}) copy-start(f32[256,512]{1,0:T(8,128)} %param.11) | copy-start | bytes 1572868
Sparse Core Ops, SparseCore 0:
  15.4 89.0 reduce-scatter.2
  112.8 49.9 reduce-scatter.4
where the time goes:
time: 172 us
  waiting for transfers between devices  139 us (81%)
  between operations  14.1 us (8%)
  other arithmetic  10.5 us (6%)
  matrix products  6.49 us (4%)
    reduce_scatter x1, waiting for transfers between devices, per_device(): lax.psum_scatter(partials.astype(jnp.bfloat16), 'fsdp', scatter_dimension...  89.1 us
    reduce_scatter x1, waiting for transfers between devices, per_device(): lax.psum_scatter(params - weights, 'replica', scatter_dimension=0, tiled=...  50.1 us
    sub x1, other arithmetic, per_device(): params - weights  8.14 us
    dot_general x1, matrix products, per_device(): lax.dot_general(sliced, key_cot[0], (((0,), (0,)), ((), ())), preferred_e...  6.49 us
  transfers between devices with their start and end apart: 2, of which 2 were waited for; matrix products, arithmetic and copies ran while one was open for 0% of the time, Pallas kernels for 0%

commit v1 on v0

v1 whole, which is shorter than its diff:
```python
import functools

import jax
import jax.numpy as jnp
from jax import lax
from jax.experimental import pallas as pl
from jax.experimental.pallas import tpu as pltpu
from jax.sharding import PartitionSpec as P

beta_one = 0.9
beta_two = 0.95
epsilon = 1e-08
inner_rate = 0.3
decay_rate = 0.1
outer_rate = 0.7
momentum = 0.9

MESH = pl.DeviceIdType.MESH
UNIT = 128


def adamw_direction(first, second, gradient):
    first = beta_one * first + (1.0 - beta_one) * gradient
    second = beta_two * second + (1.0 - beta_two) * gradient * gradient
    return first / (jnp.sqrt(second) + epsilon)


def kernel(
    n_rep, n_fsdp,
    acts_ref, cot_ref, first_ref, second_ref, total_ref,
    acts_buf, cot_buf, first_buf, second_buf, pair_out, pair_in, far_out, far_in, own_sum,
    acts_send, acts_recv, cot_send, cot_recv, pair_send, pair_recv, far_send, far_recv, state_sem, local_sem,
):
    rep = lax.axis_index("replica")
    shard = lax.axis_index("fsdp")
    n_line = n_rep // 2
    line = rep // 2
    core = lax.rem(rep, 2)
    partner = line * 2 + (1 - core)
    rows = first_ref.shape[0]
    block = rows // n_rep
    order = sorted(range(n_line), key=lambda o: (-min(o, n_line - o), -o))

    def line_of(offset):
        return lax.rem(line + offset, n_line)

    steps = []
    for k, offset in enumerate(order):
        steps.append((k, 0, line_of(offset) * 2 + (1 - core)))
        steps.append((k, 1, line_of(offset) * 2 + core))

    def rows_of(j):
        return pl.ds(pl.multiple_of(j * block, block), block)

    local = [
        pltpu.make_async_copy(cot_ref, cot_buf.at[0], local_sem.at[0]),
        pltpu.make_async_copy(
            acts_ref.at[:, pl.ds(pl.multiple_of(shard * rows, rows), rows)], acts_buf.at[0], local_sem.at[1]
        ),
    ]
    barrier = pltpu.get_barrier_semaphore()
    peers = []
    for d in range(1, n_fsdp):
        peers.append((rep, lax.rem(shard + d, n_fsdp)))
    peers.append((partner, shard))
    for o in range(1, n_line):
        peers.append((line_of(o) * 2 + core, shard))
    for peer in peers:
        pl.semaphore_signal(barrier, inc=1, device_id=peer, device_id_type=MESH)
    for copy in local:
        copy.start()
    state = []
    for i, (k, h, j) in enumerate(steps):
        pair = (
            pltpu.make_async_copy(first_ref.at[rows_of(j)], first_buf.at[rows_of(j)], state_sem.at[i, 0]),
            pltpu.make_async_copy(second_ref.at[rows_of(j)], second_buf.at[rows_of(j)], state_sem.at[i, 1]),
        )
        state.append(pair)
    pl.semaphore_wait(barrier, len(peers))

    cots = []
    for d in range(1, n_fsdp):
        copy = pltpu.make_async_remote_copy(
            src_ref=cot_ref, dst_ref=cot_buf.at[d],
            send_sem=cot_send.at[d], recv_sem=cot_recv.at[d],
            device_id=(rep, lax.rem(shard + d, n_fsdp)), device_id_type=MESH,
        )
        copy.start()
        cots.append(copy)
    moves = []
    for i, (k, h, j) in enumerate(steps):
        group = []
        for d in range(1, n_fsdp):
            target = lax.rem(shard + d, n_fsdp)
            copy = pltpu.make_async_remote_copy(
                src_ref=acts_ref.at[:, pl.ds(pl.multiple_of(target * rows + j * block, block), block)],
                dst_ref=acts_buf.at[d, :, rows_of(j)],
                send_sem=acts_send.at[i, d], recv_sem=acts_recv.at[i, d],
                device_id=(rep, target), device_id_type=MESH,
            )
            copy.start()
            group.append(copy)
        moves.append(group)
        for copy in state[i]:
            copy.start()

    for copy in local:
        copy.wait()
    for copy in cots:
        copy.wait_recv()

    tokens = acts_buf.shape[0] * acts_buf.shape[1]
    width = cot_buf.shape[2]
    sends = []
    for i, (k, h, j) in enumerate(steps):
        last = k == n_line - 1
        for copy in moves[i]:
            copy.wait_recv()
        for copy in state[i]:
            copy.wait()
        if h == 1:
            pairing.wait_recv()

        def unit(s, _, j=j, k=k, h=h, last=last):
            at = pl.ds(pl.multiple_of(j * block + s * UNIT, UNIT), UNIT)
            here = pl.ds(pl.multiple_of(s * UNIT, UNIT), UNIT)
            inputs = acts_buf[:, :, at].reshape(tokens, UNIT)
            gradient = lax.dot_general(
                inputs, cot_buf[...].reshape(tokens, width), (((0,), (0,)), ((), ())),
                preferred_element_type=jnp.float32,
            )
            value = adamw_direction(first_buf[at, :], second_buf[at, :], gradient)
            if h == 0:
                pair_out[k, here, :] = value.astype(jnp.bfloat16)
            else:
                value = value + pair_in[k, here, :].astype(jnp.float32)
                if last:
                    own_sum[here, :] = value
                else:
                    far_out[k, here, :] = value.astype(jnp.bfloat16)
            return 0

        lax.fori_loop(0, block // UNIT, unit, 0)
        if h == 0:
            pairing = pltpu.make_async_remote_copy(
                src_ref=pair_out.at[k], dst_ref=pair_in.at[k],
                send_sem=pair_send.at[k], recv_sem=pair_recv.at[k],
                device_id=(partner, shard), device_id_type=MESH,
            )
            pairing.start()
            sends.append(pairing)
        elif not last:
            copy = pltpu.make_async_remote_copy(
                src_ref=far_out.at[k], dst_ref=far_in.at[k],
                send_sem=far_send.at[k], recv_sem=far_recv.at[k],
                device_id=(j, shard), device_id_type=MESH,
            )
            copy.start()
            sends.append(copy)
            moves.append([copy])
    for group in moves[len(steps):]:
        for copy in group:
            copy.wait_recv()

    def finish(s, _):
        here = pl.ds(pl.multiple_of(s * UNIT, UNIT), UNIT)
        value = own_sum[here, :]
        for k in range(n_line - 1):
            value = value + far_in[k, here, :].astype(jnp.float32)
        total_ref[here, :] = value
        return 0

    lax.fori_loop(0, block // UNIT, finish, 0)
    for copy in cots + sends:
        copy.wait_send()
    for group in moves[: len(steps)]:
        for copy in group:
            copy.wait_send()


def fused_sum(acts, cot, first, second, n_rep, n_fsdp):
    tokens, width = cot.shape
    rows = first.shape[0]
    block = rows // n_rep
    n_line = n_rep // 2
    far = max(n_line - 1, 1)
    return pl.pallas_call(
        functools.partial(kernel, n_rep, n_fsdp),
        out_shape=jax.ShapeDtypeStruct((block, width), jnp.float32),
        in_specs=[pl.BlockSpec(memory_space=pl.ANY)] * 4,
        out_specs=pl.BlockSpec(memory_space=pltpu.VMEM),
        scratch_shapes=[
            pltpu.VMEM((n_fsdp, tokens, rows), jnp.bfloat16),
            pltpu.VMEM((n_fsdp, tokens, width), jnp.bfloat16),
            pltpu.VMEM((rows, width), jnp.float32),
            pltpu.VMEM((rows, width), jnp.float32),
            pltpu.VMEM((n_line, block, width), jnp.bfloat16),
            pltpu.VMEM((n_line, block, width), jnp.bfloat16),
            pltpu.VMEM((far, block, width), jnp.bfloat16),
            pltpu.VMEM((far, block, width), jnp.bfloat16),
            pltpu.VMEM((block, width), jnp.float32),
            pltpu.SemaphoreType.DMA((n_rep, n_fsdp)),
            pltpu.SemaphoreType.DMA((n_rep, n_fsdp)),
            pltpu.SemaphoreType.DMA((n_fsdp,)),
            pltpu.SemaphoreType.DMA((n_fsdp,)),
            pltpu.SemaphoreType.DMA((n_line,)),
            pltpu.SemaphoreType.DMA((n_line,)),
            pltpu.SemaphoreType.DMA((far,)),
            pltpu.SemaphoreType.DMA((far,)),
            pltpu.SemaphoreType.DMA((n_rep, 2)),
            pltpu.SemaphoreType.DMA((2,)),
        ],
        compiler_params=pltpu.CompilerParams(collective_id=0, has_side_effects=True),
    )(acts, cot, first, second)


def plain_sum(acts, cot, first, second):
    inputs = lax.all_to_all(acts, "fsdp", split_axis=1, concat_axis=0, tiled=True)
    cots = lax.all_gather(cot, "fsdp", axis=0, tiled=True)
    gradient = lax.dot_general(
        inputs, cots, (((0,), (0,)), ((), ())), preferred_element_type=jnp.float32
    )
    return lax.psum_scatter(
        adamw_direction(first, second, gradient), "replica", scatter_dimension=0, tiled=True
    )


def per_device(n_rep, n_fsdp, acts, key_cot, params, moment_one, moment_two, outer_mom):
    block = params.shape[0] // n_rep
    acts, key_cot = acts[0], key_cot[0]
    if block % UNIT == 0 and n_rep % 2 == 0 and n_fsdp > 1:
        total = fused_sum(acts, key_cot, moment_one, moment_two, n_rep, n_fsdp)
    else:
        total = plain_sum(acts, key_cot, moment_one, moment_two)
    anchor = lax.dynamic_slice_in_dim(params, lax.axis_index("replica") * block, block, 0)
    drift_mean = inner_rate * (total / n_rep + decay_rate * anchor)
    new_mom = momentum * outer_mom + drift_mean
    new_params = anchor - outer_rate * (drift_mean + momentum * new_mom)
    return (new_params, new_mom)


def solution(mesh):
    return jax.shard_map(
        functools.partial(per_device, mesh.shape["replica"], mesh.shape["fsdp"]),
        mesh=mesh,
        in_specs=(
            P(None, ("replica", "fsdp"), None),
            P(None, ("replica", "fsdp"), None),
            P("fsdp", None),
            P("fsdp", None),
            P("fsdp", None),
            P(("fsdp", "replica"), None),
        ),
        out_specs=(P(("fsdp", "replica"), None), P(("fsdp", "replica"), None)),
        check_vma=False,
    )
```

time: 172 us -> 49 us (0.28)
  waiting for transfers between devices: 139 us -> 0 us
  Pallas kernels: 0 us -> 45.8 us
  between operations: 14.1 us -> 0.66 us
  other arithmetic: 10.5 us -> 2.39 us
  matrix products: 6.49 us -> 0 us
    reduce_scatter x2 -> x0, waiting for transfers between devices: 139 us -> none  [the longest x1 89.1 us: per_device(): lax.psum_scatter(partials.astype(jnp.bfloat16), 'fsdp', scatter_dimension...]
    pallas_call x0 -> x1, Pallas kernels: none -> 45.8 us  [fused_sum(): pl.pallas_call(functools.partial(kernel, n_rep, n_fsdp), out_shape=jax.Sh...]
    sub x1 -> x0, other arithmetic: 8.14 us -> none  [per_device(): params - weights]
    dot_general x1 -> x0, matrix products: 6.49 us -> none  [per_device(): lax.dot_general(sliced, key_cot[0], (((0,), (0,)), ((), ())), preferred_e...]
  transfers between devices with their start and end apart: 2 -> 0, of which waited for: 2 -> 0; matrix products, arithmetic and copies ran while one was open for 0% -> 0% of each run, Pallas kernels for 0% -> 0%
where the time goes in v1:
time: 49 us; the launch traced here: 48.9 us
  Pallas kernels  45.8 us (93%)
  other arithmetic  2.39 us (5%)
  between operations  0.66 us (1%)
    pallas_call x1, Pallas kernels, fused_sum(): pl.pallas_call(functools.partial(kernel, n_rep, n_fsdp), out_shape=jax.Sh...  45.8 us
    sub x1, other arithmetic, per_device(): new_params = anchor - outer_rate * (drift_mean + momentum * new_mom)  2.39 us

profile of v1, /device:TPU:0, one launch (start us, length us, event | category | flops | bytes accessed | tf_op | source)
XLA Modules:
  0.0 48.9 jit_solution(18173234992574574490)
XLA Ops:
  0.6 0.0 copy-start
  0.6 45.8 %shard_map.77 = f32[256,512]{1,0:T(8,128)} custom-call(bf16[128,8192]{1,0:T(8,128)(2,1)} %bitcast.2, bf16[128,512]{1,0:T(8,128)(2,1)} %bitcast.3, f32[2048,512]{1,0:T(8,128)} %first_ref.1, f32[2048,512]{1,0:T(8,128)} %second_ref.1), custom_call_target="tpu_custom_call" | custom-call | tf_op jit(solution)/shard_map/pallas_call | solution.py:187
  46.5 0.0 copy-done
  46.5 2.4 %multiply_subtract_fusion = (f32[256,512]{1,0:T(8,128)}, f32[256,512]{1,0:T(8,128)}) fusion(f32[2048,512]{1,0:T(8,128)} %param.8, s32[]{:T(128)S(6)} %select_n.3, f32[256,512]{1,0:T(8,128)} %shard_map.77, f32[256,512]{1,0:T(8,128)S(1)} %copy-done), kind=kLoop, calls=%fused_computation | loop fusion | flops 1310720 | bytes 2621444 | tf_op jit(solution)/shard_map/sub | solution.py:238
Async XLA Ops:
  0.6 45.8 %copy-start = (f32[256,512]{1,0:T(8,128)S(1)}, f32[256,512]{1,0:T(8,128)}, u32[]{:S(2)}) copy-start(f32[256,512]{1,0:T(8,128)} %param.11) | copy-start | bytes 1572868

commit v2 on v0

v2 whole, which is shorter than its diff:
```python
import functools

import jax
import jax.numpy as jnp
from jax import lax
from jax.experimental import pallas as pl
from jax.experimental.pallas import tpu as pltpu
from jax.sharding import PartitionSpec as P

beta_one = 0.9
beta_two = 0.95
epsilon = 1e-08
inner_rate = 0.3
decay_rate = 0.1
outer_rate = 0.7
momentum = 0.9

MESH = pl.DeviceIdType.MESH
UNIT = 128

def adamw_direction(first, second, gradient):
    first = beta_one * first + (1.0 - beta_one) * gradient
    second = beta_two * second + (1.0 - beta_two) * gradient * gradient
    return first / (jnp.sqrt(second) + epsilon)

def kernel(
    n_rep, splits,
    acts_ref, cot_ref, params_ref, first_ref, second_ref, outer_ref, new_params_ref, new_mom_ref,
    acts_buf, cot_buf, first_buf, second_buf, pair_out, pair_in, far_out, far_in, own_sum, anchor_buf, outer_buf,
    acts_send, acts_recv, cot_send, cot_recv, pair_send, pair_recv, far_send, far_recv, state_sem, local_sem,
):
    rep = lax.axis_index("replica")
    shard = lax.axis_index("fsdp")
    line, core = lax.div(rep, 2), lax.rem(rep, 2)
    row_at, col_at = lax.div(shard, 2), lax.rem(shard, 2)
    rows = first_ref.shape[0]
    block = rows // n_rep
    half = cot_ref.shape[0] // 2
    tokens = acts_buf.shape[0] * acts_buf.shape[1]
    width = cot_buf.shape[2]
    partner = line * 2 + (1 - core)
    shards = (shard, row_at * 2 + (1 - col_at), (1 - row_at) * 2 + col_at, (1 - row_at) * 2 + (1 - col_at))
    lines = (line, line + 1 - 2 * lax.rem(line, 2), lax.rem(line + 2, 4), 3 - line)
    outer = 1 - lax.rem(lax.div(line, 2) + lax.rem(line, 2), 2)
    is_outer = outer == 1
    n_line = len(lines)

    units = []
    for k in range(n_line):
        other = lines[n_line - 1 - k]
        size = block // splits[k]
        for h, owner in ((0, 1 - core), (1, core)):
            for part in range(splits[k]):
                units.append((k, part * size, size, h, other * 2 + owner))

    def span(start, size):
        return pl.ds(pl.multiple_of(start, size), size)

    def remote(source, target, send, recv, device):
        return pltpu.make_async_remote_copy(
            src_ref=source, dst_ref=target, send_sem=send, recv_sem=recv, device_id=device, device_id_type=MESH
        )

    local = [
        pltpu.make_async_copy(cot_ref, cot_buf.at[0], local_sem.at[0]),
        pltpu.make_async_copy(acts_ref.at[:, span(shard * rows, rows)], acts_buf.at[0], local_sem.at[1]),
    ]
    state = []
    for i, (k, start, size, h, j) in enumerate(units):
        at = span(j * block + start, size)
        state.append((
            pltpu.make_async_copy(first_ref.at[at], first_buf.at[at], state_sem.at[i, 0]),
            pltpu.make_async_copy(second_ref.at[at], second_buf.at[at], state_sem.at[i, 1]),
        ))
    barrier = pltpu.get_barrier_semaphore()
    peers = [(rep, shards[d]) for d in range(1, 4)] + [(partner, shard)]
    peers += [(lines[o] * 2 + core, shard) for o in (1, 2)]
    for peer in peers:
        pl.semaphore_signal(barrier, inc=1, device_id=peer, device_id_type=MESH)

    @pl.when(jnp.logical_not(is_outer))
    def _():
        pl.semaphore_signal(barrier, inc=1, device_id=(lines[3] * 2 + core, shard), device_id_type=MESH)

    for copy in local:
        copy.start()
    pl.semaphore_wait(barrier, len(peers) + 1 - outer)

    sends = []
    cots = []
    for d in (1, 2):
        copy = remote(cot_ref, cot_buf.at[d], cot_send.at[d], cot_recv.at[d], (rep, shards[d]))
        copy.start()
        cots.append(copy)
    moves = []

    def issue(i):
        k, start, size, h, j = units[i]
        group = []
        for d in (3, 1, 2):
            copy = remote(
                acts_ref.at[:, span(shards[d] * rows + j * block + start, size)],
                acts_buf.at[d, :, span(j * block + start, size)],
                acts_send.at[i, d], acts_recv.at[i, d], (rep, shards[d]),
            )
            copy.start()
            group.append(copy)
        moves.append(group)
        for copy in state[i]:
            copy.start()

    for i in range(2):
        issue(i)
    for d, via in ((1, 2), (2, 1)):
        cots[d - 1].wait_recv()
        piece = pl.ds((d - 1) * half, half)
        copy = remote(
            cot_buf.at[d, piece], cot_buf.at[3, piece], cot_send.at[d + 2], cot_recv.at[d + 2], (rep, shards[via])
        )
        copy.start()
        cots.append(copy)
    for i in range(2, len(units)):
        issue(i)
    finals = [
        pltpu.make_async_copy(params_ref.at[span(rep * block, block)], anchor_buf, local_sem.at[2]),
        pltpu.make_async_copy(outer_ref, outer_buf, local_sem.at[3]),
    ]
    for copy in finals:
        copy.start()
    for copy in local:
        copy.wait()
    for copy in cots[2:]:
        copy.wait_recv()

    far_sends = []
    pairings = {}
    for i, (k, start, size, h, j) in enumerate(units):
        last = k == n_line - 1
        for copy in moves[i]:
            copy.wait_recv()
        for copy in state[i]:
            copy.wait()
        at = span(j * block + start, size)
        here = pl.ds(start, size)
        gradient = lax.dot_general(
            acts_buf[:, :, at].reshape(tokens, size), cot_buf[...].reshape(tokens, width),
            (((0,), (0,)), ((), ())), preferred_element_type=jnp.float32,
        )
        value = adamw_direction(first_buf[at, :], second_buf[at, :], gradient)
        sem = (k, start // size)
        if h == 0:
            pair_out[k, here, :] = value
            pairing = remote(
                pair_out.at[k, here], pair_in.at[k, here], pair_send.at[sem], pair_recv.at[sem], (partner, shard)
            )
            pairing.start()
            pairings[sem] = pairing
            sends.append(pairing)
            continue
        pairings[sem].wait_recv()
        value = value + pair_in[k, here, :]
        if last:
            own_sum[here, :] = value
            continue
        if k == 0:
            slot = outer * 3
            device = ((outer * lines[1] + (1 - outer) * lines[3]) * 2 + core, shard)
        else:
            slot = k
            device = (j, shard)
        if k == 1:
            arrival = remote(
                far_out.at[k, here], far_in.at[3, here],
                far_send.at[3, start // size], far_recv.at[3, start // size], device,
            )

            @pl.when(is_outer)
            def _(value=value, k=k, here=here):
                far_out[k, here, :] = value.astype(jnp.bfloat16)

            @pl.when(jnp.logical_not(is_outer))
            def _(value=value, k=k, here=here, arrival=arrival):
                arrival.wait_recv()
                far_out[k, here, :] = (value + far_in[3, here, :].astype(jnp.float32)).astype(jnp.bfloat16)
        else:
            far_out[k, here, :] = value.astype(jnp.bfloat16)
        copy = remote(
            far_out.at[k, here], far_in.at[slot, here],
            far_send.at[sem], far_recv.at[slot, start // size], device,
        )
        copy.start()
        far_sends.append((k, start, size, copy))

    for k, start, size, copy in far_sends:
        if k > 0:
            copy.wait_recv()
        else:
            arrival = remote(
                far_out.at[0, pl.ds(start, size)], far_in.at[0, pl.ds(start, size)],
                far_send.at[0, start // size], far_recv.at[0, start // size], (rep, shard),
            )

            @pl.when(jnp.logical_not(is_outer))
            def _(arrival=arrival):
                arrival.wait_recv()

    @pl.when(jnp.logical_not(is_outer))
    def _():
        own_sum[...] = own_sum[...] + far_in[0].astype(jnp.float32)

    for copy in finals:
        copy.wait()
    anchor = anchor_buf[...]
    total = own_sum[...] + (far_in[1].astype(jnp.float32) + far_in[2].astype(jnp.float32))
    drift_mean = inner_rate * (total / n_rep + decay_rate * anchor)
    new_mom = momentum * outer_buf[...] + drift_mean
    new_params_ref[...] = anchor - outer_rate * (drift_mean + momentum * new_mom)
    new_mom_ref[...] = new_mom

    for copy in cots + sends + [entry[3] for entry in far_sends]:
        copy.wait_send()
    for group in moves:
        for copy in group:
            copy.wait_send()

def fused_round(acts, cot, params, first, second, outer, n_rep, n_fsdp):
    tokens, width = cot.shape
    rows = first.shape[0]
    block = rows // n_rep
    n_line = n_rep // 2
    splits = (block // UNIT,) * n_line
    units = 2 * sum(splits)
    parts = max(splits)
    return pl.pallas_call(
        functools.partial(kernel, n_rep, splits),
        out_shape=(pltpu.VMEM((block, width), jnp.float32),) * 2,
        in_specs=[pl.BlockSpec(memory_space=pltpu.HBM)] * 6,
        out_specs=(pl.BlockSpec(memory_space=pltpu.VMEM),) * 2,
        scratch_shapes=[
            pltpu.VMEM((n_fsdp, tokens, rows), jnp.bfloat16),
            pltpu.VMEM((n_fsdp, tokens, width), jnp.bfloat16),
            pltpu.VMEM((rows, width), jnp.float32),
            pltpu.VMEM((rows, width), jnp.float32),
            pltpu.VMEM((n_line, block, width), jnp.float32),
            pltpu.VMEM((n_line, block, width), jnp.float32),
            pltpu.VMEM((n_line, block, width), jnp.bfloat16),
            pltpu.VMEM((n_line, block, width), jnp.bfloat16),
            pltpu.VMEM((block, width), jnp.float32),
            pltpu.VMEM((block, width), jnp.float32),
            pltpu.VMEM((block, width), jnp.float32),
            pltpu.SemaphoreType.DMA((units, n_fsdp)),
            pltpu.SemaphoreType.DMA((units, n_fsdp)),
            pltpu.SemaphoreType.DMA((5,)),
            pltpu.SemaphoreType.DMA((5,)),
            pltpu.SemaphoreType.DMA((n_line, parts)),
            pltpu.SemaphoreType.DMA((n_line, parts)),
            pltpu.SemaphoreType.DMA((n_line, parts)),
            pltpu.SemaphoreType.DMA((n_line, parts)),
            pltpu.SemaphoreType.DMA((units, 2)),
            pltpu.SemaphoreType.DMA((4,)),
        ],
        compiler_params=pltpu.CompilerParams(collective_id=0, has_side_effects=True),
    )(acts, cot, params, first, second, outer)

def plain_sum(acts, cot, first, second):
    inputs = lax.all_to_all(acts, "fsdp", split_axis=1, concat_axis=0, tiled=True)
    cots = lax.all_gather(cot, "fsdp", axis=0, tiled=True)
    gradient = lax.dot_general(
        inputs, cots, (((0,), (0,)), ((), ())), preferred_element_type=jnp.float32
    )
    return lax.psum_scatter(
        adamw_direction(first, second, gradient), "replica", scatter_dimension=0, tiled=True
    )

def per_device(n_rep, n_fsdp, acts, key_cot, params, moment_one, moment_two, outer_mom):
    block = params.shape[0] // n_rep
    acts, key_cot = acts[0], key_cot[0]
    if block % UNIT == 0 and n_rep == 8 and n_fsdp == 4:
        return fused_round(acts, key_cot, params, moment_one, moment_two, outer_mom, n_rep, n_fsdp)
    total = plain_sum(acts, key_cot, moment_one, moment_two)
    anchor = lax.dynamic_slice_in_dim(params, lax.axis_index("replica") * block, block, 0)
    drift_mean = inner_rate * (total / n_rep + decay_rate * anchor)
    new_mom = momentum * outer_mom + drift_mean
    new_params = anchor - outer_rate * (drift_mean + momentum * new_mom)
    return (new_params, new_mom)

def solution(mesh):
    return jax.shard_map(
        functools.partial(per_device, mesh.shape["replica"], mesh.shape["fsdp"]),
        mesh=mesh,
        in_specs=(
            P(None, ("replica", "fsdp"), None),
            P(None, ("replica", "fsdp"), None),
            P("fsdp", None),
            P("fsdp", None),
            P("fsdp", None),
            P(("fsdp", "replica"), None),
        ),
        out_specs=(P(("fsdp", "replica"), None), P(("fsdp", "replica"), None)),
        check_vma=False,
    )
```

time: 172 us -> 45.5 us (0.26)
  waiting for transfers between devices: 139 us -> 0 us
  Pallas kernels: 0 us -> 43.2 us
  between operations: 14.1 us -> 0.64 us
  other arithmetic: 10.5 us -> 0 us
  matrix products: 6.49 us -> 0 us
    reduce_scatter x2 -> x0, waiting for transfers between devices: 139 us -> none  [the longest x1 89.1 us: per_device(): lax.psum_scatter(partials.astype(jnp.bfloat16), 'fsdp', scatter_dimension...]
    pallas_call x0 -> x1, Pallas kernels: none -> 43.2 us  [fused_round(): pl.pallas_call(functools.partial(kernel, n_rep, splits), out_shape=(pltpu...]
    sub x2 -> x0, other arithmetic: 10.5 us -> none  [the longest x1 8.14 us: per_device(): params - weights]
    dot_general x1 -> x0, matrix products: 6.49 us -> none  [per_device(): lax.dot_general(sliced, key_cot[0], (((0,), (0,)), ((), ())), preferred_e...]
  transfers between devices with their start and end apart: 2 -> 0, of which waited for: 2 -> 0; matrix products, arithmetic and copies ran while one was open for 0% -> 0% of each run, Pallas kernels for 0% -> 0%
where the time goes in v2:
time: 45.5 us; the launch traced here: 45.4 us
  Pallas kernels  43.2 us (95%)
  local copies, waits for them, and re-layouts  1.59 us (3%)
  between operations  0.64 us (1%)
    pallas_call x1, Pallas kernels, fused_round(): pl.pallas_call(functools.partial(kernel, n_rep, splits), out_shape=(pltpu...  43.2 us
    unnamed x2, local copies, waits for them, and re-layouts  1.59 us

profile of v2, /device:TPU:0, one launch (start us, length us, event | category | flops | bytes accessed | tf_op | source)
XLA Modules:
  0.0 45.4 jit_solution(13441906706739133985)
XLA Ops:
  0.6 43.2 %shard_map.77 = (f32[256,512]{1,0:T(8,128)S(1)}, f32[256,512]{1,0:T(8,128)S(1)}) custom-call(bf16[128,8192]{1,0:T(8,128)(2,1)} %bitcast.2, bf16[128,512]{1,0:T(8,128)(2,1)} %bitcast.3, f32[2048,512]{1,0:T(8,128)} %params_ref.1, f32[2048,512]{1,0:T(8,128)} %first_ref.1, f32[2048,512]{1,0:T(8,128)} %second_ref.1, f32[256,512]{1,0:T(8,128)} %outer_ref.1), custom_call_target="tpu_custom_call" | custom-call | tf_op jit(solution)/shard_map/pallas_call | solution.py:234
  43.8 0.8 %copy.10 = f32[256,512]{1,0:T(8,128)} copy(f32[256,512]{1,0:T(8,128)S(1)} %get-tuple-element.2) | data formatting | bytes 1048576
  44.6 0.8 %copy.11 = f32[256,512]{1,0:T(8,128)} copy(f32[256,512]{1,0:T(8,128)S(1)} %get-tuple-element.3) | data formatting | bytes 1048576

commit v3 on v2

--- a/solution.py
+++ b/solution.py
@@ -17,6 +17,7 @@
 
 MESH = pl.DeviceIdType.MESH
 UNIT = 128
+WINDOW = 4
 
 def adamw_direction(first, second, gradient):
     first = beta_one * first + (1.0 - beta_one) * gradient
@@ -119,7 +120,7 @@
         )
         copy.start()
         cots.append(copy)
-    for i in range(2, len(units)):
+    for i in range(2, WINDOW):
         issue(i)
     finals = [
         pltpu.make_async_copy(params_ref.at[span(rep * block, block)], anchor_buf, local_sem.at[2]),
@@ -138,6 +139,8 @@
         last = k == n_line - 1
         for copy in moves[i]:
             copy.wait_recv()
+        if i + WINDOW < len(units):
+            issue(i + WINDOW)
         for copy in state[i]:
             copy.wait()
         at = span(j * block + start, size)

time: 45.5 us -> 44.6 us (0.980)
  Pallas kernels: 43.2 us -> 42.2 us
    pallas_call x1, Pallas kernels: 43.2 us -> 42.2 us  [fused_round(): pl.pallas_call(functools.partial(kernel, n_rep, splits), out_shape=(pltpu...]
where the time goes in v3:
time: 44.6 us; the launch traced here: 44.5 us
  Pallas kernels  42.2 us (95%)
  local copies, waits for them, and re-layouts  1.59 us (4%)
  between operations  0.64 us (1%)
    pallas_call x1, Pallas kernels, fused_round(): pl.pallas_call(functools.partial(kernel, n_rep, splits), out_shape=(pltpu...  42.2 us
    unnamed x2, local copies, waits for them, and re-layouts  1.59 us

profile of v3, /device:TPU:0, one launch (start us, length us, event | category | flops | bytes accessed | tf_op | source)
XLA Modules:
  0.0 44.5 jit_solution(5848822042365047959)
XLA Ops:
  0.6 42.2 %shard_map.77 = (f32[256,512]{1,0:T(8,128)S(1)}, f32[256,512]{1,0:T(8,128)S(1)}) custom-call(bf16[128,8192]{1,0:T(8,128)(2,1)} %bitcast.2, bf16[128,512]{1,0:T(8,128)(2,1)} %bitcast.3, f32[2048,512]{1,0:T(8,128)} %params_ref.1, f32[2048,512]{1,0:T(8,128)} %first_ref.1, f32[2048,512]{1,0:T(8,128)} %second_ref.1, f32[256,512]{1,0:T(8,128)} %outer_ref.1), custom_call_target="tpu_custom_call" | custom-call | tf_op jit(solution)/shard_map/pallas_call | solution.py:237
  42.9 0.8 %copy.10 = f32[256,512]{1,0:T(8,128)} copy(f32[256,512]{1,0:T(8,128)S(1)} %get-tuple-element.2) | data formatting | bytes 1048576
  43.7 0.8 %copy.11 = f32[256,512]{1,0:T(8,128)} copy(f32[256,512]{1,0:T(8,128)S(1)} %get-tuple-element.3) | data formatting | bytes 1048576
